TPU v7x, 32 devices: a whole 2x2x4 slice. The times are simulated.
32 devices in a mesh: row: 16 (over z, x, core), col: 2 (over y).
Axes of the slice: x: 2, y: 2, z: 4, core: 2. Of those that a mesh axis runs over, the one named last changes fastest.
Arguments:
- vectors: bfloat16 [8, 4096], P(None, ('row', 'col')), may hold values from -16 to 16, as said below
- tile_vals: bfloat16 [16, 2, 3, 4, 128, 128], P('row', 'col'), may hold values from -0.375 to 0.375
- tile_rows: int32 [16, 2, 3, 4], P('row', 'col'), may hold values from 0 to 1, as said below
- tile_cols: int32 [16, 2, 3, 4], P('row', 'col'), may hold values from 0 to 15, as said below
- tile_counts: int32 [16, 2, 3], P('row', 'col'), may hold values from 1 to 4, as said below
- tile_diag: int32 [16, 2, 3, 4], P('row', 'col'), may hold values from 0 to 1, as said below
Outputs:
- applied: float32 [3, 8, 4096], P(None, None, ('row', 'col'))
- subspace: float32 [3, 8, 8], replicated
Inputs may be any that keep to these rules, and one draw needn't show every extreme that they name: `vectors`: eigenvector amplitudes vary over the basis. `tile_rows`: the first tile_counts slots of a term on a device name distinct tiles whose global tile row is at least the global tile column; later slots are ignored. `tile_cols`: see tile_rows. `tile_counts`: loads differ from device to device. `tile_diag`: 1 exactly for live slots whose global tile row equals the global tile column, else 0.
All inputs are finite; a program needn't handle non-finite values.
Results may differ from a plain program's by a relative error of at most 0.0003.
Values may be sent and summed in bfloat16 or wider, within the bound.
A program may use at most 64 MiB of HBM per device.

v0:
```python
import math

import jax
import jax.numpy as jnp
from jax import lax
from jax.sharding import PartitionSpec as P


def place_terms(tiles_now, rows_now, cols_now, live_wt, mirror_wt, row_segs, col_segs):
    vec_count = row_segs.shape[0]
    row_tiles = row_segs.shape[1]
    col_tiles = col_segs.shape[1]
    width = row_segs.shape[2]
    picked_cols = jnp.take(col_segs, cols_now, axis=1)
    forward_terms = jnp.einsum(
        "kij,ekj->eki", tiles_now, picked_cols, preferred_element_type=jnp.float32
    )
    row_hot = (rows_now[None, :] == jnp.arange(row_tiles, dtype=jnp.int32)[:, None]).astype(
        jnp.float32
    ) * live_wt[None, :]
    forward_part = jnp.einsum(
        "ak,eki->eai", row_hot, forward_terms, precision=lax.Precision.HIGHEST
    )
    picked_rows = jnp.take(row_segs, rows_now, axis=1)
    mirror_terms = jnp.einsum(
        "kij,eki->ekj", tiles_now, picked_rows, preferred_element_type=jnp.float32
    )
    col_hot = (cols_now[None, :] == jnp.arange(col_tiles, dtype=jnp.int32)[:, None]).astype(
        jnp.float32
    ) * mirror_wt[None, :]
    mirror_part = jnp.einsum("bk,ekj->ebj", col_hot, mirror_terms, precision=lax.Precision.HIGHEST)
    return (
        forward_part.reshape(vec_count, row_tiles * width),
        mirror_part.reshape(vec_count, col_tiles * width),
    )


def shards(vectors, tile_vals, tile_rows, tile_cols, tile_counts, tile_diag):
    vec_count = vectors.shape[0]
    piece = vectors.shape[1]
    width = tile_vals.shape[-1]
    slots = tile_vals.shape[3]
    term_count = tile_vals.shape[2]
    row_block = lax.all_gather(vectors, "col", axis=1, tiled=True)
    col_block = lax.all_gather(vectors, "row", axis=1, tiled=True)
    row_segs = row_block.reshape(vec_count, -1, width)
    col_segs = col_block.reshape(vec_count, -1, width)
    slot_ids = jnp.arange(slots, dtype=jnp.int32)
    forward_list = []
    mirror_list = []
    for term_idx in range(term_count):
        live_wt = (slot_ids < tile_counts[0, 0, term_idx]).astype(jnp.float32)
        mirror_wt = live_wt * (1 - tile_diag[0, 0, term_idx]).astype(jnp.float32)
        forward_part, mirror_part = place_terms(
            tile_vals[0, 0, term_idx],
            tile_rows[0, 0, term_idx],
            tile_cols[0, 0, term_idx],
            live_wt,
            mirror_wt,
            row_segs,
            col_segs,
        )
        forward_list.append(forward_part)
        mirror_list.append(mirror_part)
    forward_sums = lax.psum_scatter(jnp.stack(forward_list), "col", scatter_dimension=2, tiled=True)
    mirror_sums = lax.psum_scatter(jnp.stack(mirror_list), "row", scatter_dimension=2, tiled=True)
    applied = forward_sums + mirror_sums
    local_terms = jnp.einsum(
        "ei,tfi->tef", vectors.astype(jnp.float32), applied, precision=lax.Precision.HIGHEST
    )
    summed = jnp.stack(
        [lax.psum(local_terms[term_idx], ("row", "col")) for term_idx in range(term_count)]
    )
    total_states = piece * lax.axis_size("row") * lax.axis_size("col")
    return (applied, summed / math.sqrt(total_states))


def solution(mesh):
    placed = (
        P(None, ("row", "col")),
        P("row", "col", None, None, None, None),
        P("row", "col", None, None),
        P("row", "col", None, None),
        P("row", "col", None),
        P("row", "col", None, None),
    )
    return jax.shard_map(
        shards,
        mesh=mesh,
        in_specs=placed,
        out_specs=(P(None, None, ("row", "col")), P()),
        check_vma=False,
    )
```

profile of v0, /device:TPU:0, one launch (start us, length us, event | category | flops | bytes accessed | tf_op | source)
XLA Modules:
  0.0 153.4 jit_solution(7228136730553629961)
XLA Ops:
  7.2 1.4 fusion.101
  8.6 23.4 %all_gather.6 = bf16[8,2048]{1,0:T(8,128)(2,1)S(1)} all-gather(bf16[8,128]{1,0:T(8,128)(2,1)} %param.10), channel_id=1, replica_groups=mesh['row'=16,'col'=2] {'row'}, dimensions={1}, use_global_device_ids=true | all-gather | bytes 34816 | tf_op jit(solution)/shard_map/all_gather | solution.py:45
  32.0 0.6 compare_convert_fusion.1
  32.6 0.7 slice_bitcast_fusion.4
  33.3 0.6 gather_fusion.1
  33.9 1.1 fusion.6
  35.2 0.6 gather_fusion.2
  35.7 0.7 compare_convert_fusion
  36.4 1.1 fusion.2
  37.5 0.2 convolution_bitcast_fusion.4
  37.7 0.6 gather_fusion
  38.3 0.7 compare_convert_fusion.2
  39.4 0.6 pad_maximum_fusion.1
  40.1 0.6 copy-done.3
  40.7 4.4 %all_gather.7 = bf16[8,256]{1,0:T(8,128)(2,1)S(1)} all-gather(bf16[8,128]{1,0:T(8,128)(2,1)S(1)} %copy-done.2), channel_id=1, replica_groups=mesh['row'=16,'col'=2] {'col'}, dimensions={1}, use_global_device_ids=true | all-gather | bytes 6144 | tf_op jit(solution)/shard_map/all_gather | solution.py:44
  45.0 0.7 copy-done.5
  45.7 1.9 %compare_select_fusion.11 = (f32[4]{0:T(128)S(1)}, f32[4]{0:T(128)S(1)}, f32[4]{0:T(128)S(1)}) fusion(s32[1,1,3,4]{3,1,2,0:T(1,128)S(1)} %copy-done.5, s32[]{:T(128)} %bitcast.6, s32[]{:T(128)} %bitcast.22, s32[]{:T(128)} %bitcast.14), kind=kLoop, calls=%fused_computation.105 | loop fusion | flops 48 | bytes 108 | tf_op jit(solution)/shard_map/mul | solution.py:53
  47.6 0.6 gather_fusion.4
  48.2 0.2 fusion.4
  48.4 0.3 convolution_bitcast_fusion.1
  48.7 0.6 gather_fusion.5
  49.3 0.2 fusion
  49.5 0.3 convolution_bitcast_fusion
  49.9 0.6 gather_fusion.3
  50.4 0.2 fusion.8
  50.6 0.3 convolution_bitcast_fusion.2
  51.0 0.7 pad_maximum_fusion
  51.7 52.6 %reduce-scatter.5.cloned.1.call-done = f32[3,8,128]{2,1,0:T(8,128)} async-done(((f32[3,8,2048]{2,1,0:T(8,128)}), f32[3,8,128]{2,1,0:T(8,128)}) %reduce-scatter.5.cloned.1.call-update) | async-done | bytes 12304 | tf_op jit(solution)/shard_map/reduce_scatter | solution.py:66
  104.3 0.7 add.19
  105.2 0.5 copy-done.1
  105.6 40.2 %all-reduce = (f32[1,8,8]{1,2,0:T(8,128)S(1)}, f32[1,8,8]{1,2,0:T(8,128)S(1)}, f32[1,8,8]{1,2,0:T(8,128)S(1)}) all-reduce(f32[1,8,8]{1,2,0:T(8,128)S(1)} %get-tuple-element.22, f32[1,8,8]{1,2,0:T(8,128)S(1)} %get-tuple-element.23, f32[1,8,8]{1,2,0:T(8,128)S(1)} %get-tuple-element.21), channel_id=1, replica_groups=mesh['row'=16,'col'=2] {'row','col'}, use_global_device_ids=true, to_apply=%region_4.7 | all-reduce | flops 192 | bytes 1536 | tf_op jit(solution)/shard_map/psum | solution.py:72
  145.9 0.7 copy.8
  (33 shorter events, 1.0 us)
Async XLA Ops:
  7.2 1.4 copy-start.4
  7.2 31.8 %copy-start = (bf16[1,1,3,4,128,128]{5,4,3,2,1,0:T(8,128)(2,1)S(1)}, bf16[1,1,3,4,128,128]{5,4,3,2,1,0:T(8,128)(2,1)}, u32[]{:S(2)}) copy-start(bf16[1,1,3,4,128,128]{5,4,3,2,1,0:T(8,128)(2,1)} %param.11) | copy-start | bytes 1179652
  7.2 44.5 %reduce-scatter.3.cloned.1.call-start = ((), (), s32[]{:S(2)}) async-start(), calls=%async_computation.2 | async-start | bytes 36864 | tf_op jit(solution)/shard_map/reduce_scatter | solution.py:65
  40.0 0.7 copy-start.3
  40.0 0.7 copy-start.2
  40.0 64.3 %reduce-scatter.5.cloned.1.call-start = ((), (), s32[]{:S(2)}) async-start(), calls=%async_computation.3 | async-start | bytes 208896 | tf_op jit(solution)/shard_map/reduce_scatter | solution.py:66
  45.0 0.7 copy-start.5
  105.0 0.6 copy-start.1
Sparse Core Ops, SparseCore 0:
  40.1 7.2 reduce-scatter.2
  51.8 52.4 reduce-scatter.4
where the time goes:
time: 154 us; the launch traced here: 153 us
  blocking collectives  68 us (44%)
  waiting for transfers between devices  52.6 us (34%)
  between operations  14.2 us (9%)
  local copies, waits for them, and re-layouts  7.96 us (5%)
  other arithmetic  5.79 us (4%)
  matrix products  4.7 us (3%)
    reduce_scatter x1, waiting for transfers between devices, shards(): lax.psum_scatter(jnp.stack(mirror_list), 'row', scatter_dimension=2, tile...  52.6 us
    psum x1, blocking collectives, shards(): lax.psum(local_terms[term_idx], ('row', 'col'))  40.2 us
    all_gather x1, blocking collectives, shards(): col_block = lax.all_gather(vectors, 'row', axis=1, tiled=True)  23.4 us
    all_gather x1, blocking collectives, shards(): row_block = lax.all_gather(vectors, 'col', axis=1, tiled=True)  4.35 us
  transfers between devices with their start and end apart: 2, of which 1 were waited for; matrix products, arithmetic and copies ran while one was open for 4% of the time, Pallas kernels for 0%

commit v1 on v0

v1 whole, which is shorter than its diff:
```python
import functools
import math

import jax
import jax.numpy as jnp
from jax import lax
from jax.experimental import pallas as pl
from jax.experimental.pallas import tpu as pltpu
from jax.sharding import PartitionSpec as P

MESH = pl.DeviceIdType.MESH
HIGHEST = lax.Precision.HIGHEST
LAST = (((1,), (1,)), ((), ()))


def kernel(
    nr, nc, scale,
    v_ref, w_hbm, rows, cols, counts, diag,
    app_ref, sub_ref,
    w, rowv, colv, mterm, mpart, mrecv, fpart, frecv, ssend, srecv,
    w_sem, rv_send, rv_recv, cv_send, cv_recv, m_send, m_recv, f_send, f_recv, s_send, s_recv,
):
    r = lax.axis_index("row")
    c = lax.axis_index("col")
    ev, width = v_ref.shape
    terms, slots = w.shape[0], w.shape[1]
    top = terms * ev

    def remote(src, dst, send, recv, row, col):
        return pltpu.make_async_remote_copy(
            src_ref=src, dst_ref=dst, send_sem=send, recv_sem=recv,
            device_id=(row, col), device_id_type=MESH,
        )

    def each_row(fn):
        @pl.loop(1, nr)
        def _(d):
            fn(lax.rem(r + d, nr))

    def each_col(fn):
        @pl.loop(1, nc)
        def _(d):
            fn(lax.rem(c + d, nc))

    w_copy = pltpu.make_async_copy(w_hbm.at[0, 0], w, w_sem)
    w_copy.start()

    barrier = pltpu.get_barrier_semaphore()
    each_row(lambda p: pl.semaphore_signal(barrier, inc=1, device_id=(p, c), device_id_type=MESH))
    each_col(lambda p: pl.semaphore_signal(barrier, inc=1, device_id=(r, p), device_id_type=MESH))
    own = v_ref[...]
    rowv[c] = own
    colv[r] = own

    @pl.loop(r + 1, nr)
    def _(b):
        colv[b] = jnp.zeros_like(own)

    pl.semaphore_wait(barrier, nr - 1 + nc - 1)

    def rv(p):
        return remote(v_ref, rowv.at[c], rv_send.at[p], rv_recv.at[c], r, p)

    def cv(p):
        return remote(v_ref, colv.at[r], cv_send.at[p], cv_recv.at[r], p, c)

    each_col(lambda p: rv(p).start())

    @pl.loop(0, nr - 1 - r)
    def _(i):
        cv(nr - 1 - i).start()

    w_copy.wait()
    each_col(lambda p: remote(v_ref, rowv.at[p], rv_send.at[p], rv_recv.at[p], r, p).wait_recv())

    live = []
    off = []
    for t in range(terms):
        for k in range(slots):
            alive = k < counts[0, 0, t]
            live.append(jnp.where(alive, 1.0, 0.0).astype(jnp.float32))
            off.append(jnp.where(alive & (diag[0, t, 0, k] == 0), 1.0, 0.0).astype(jnp.float32))
            mterm[t, k] = jnp.dot(
                rowv[rows[0, t, 0, k]], w[t, k], preferred_element_type=jnp.float32
            )

    @pl.loop(0, r + 1)
    def _(b):
        for t in range(terms):
            total = jnp.zeros((ev, width), jnp.float32)
            for k in range(slots):
                weight = jnp.where(cols[0, t, 0, k] == b, off[t * slots + k], 0.0)
                total += weight * mterm[t, k]
            mpart[b, t] = total

    def mp(b):
        return remote(mpart.at[b], mrecv.at[r], m_send.at[b], m_recv.at[r], b, c)

    @pl.loop(0, r)
    def _(b):
        mp(b).start()

    @pl.loop(0, r)
    def _(b):
        remote(v_ref, colv.at[b], cv_send.at[b], cv_recv.at[b], b, c).wait_recv()

    forward = []
    small = []
    for t in range(terms):
        seen = []
        for k in range(slots):
            seen.append(colv[jnp.minimum(cols[0, t, 0, k], r)])
            forward.append(
                lax.dot_general(seen[k], w[t, k], LAST, preferred_element_type=jnp.float32)
                * live[t * slots + k]
            )
        wide = jnp.concatenate(seen, axis=1).astype(jnp.float32)
        ahead = jnp.concatenate([mterm[t, k] * live[t * slots + k] for k in range(slots)], axis=1)
        back = jnp.concatenate([mterm[t, k] * off[t * slots + k] for k in range(slots)], axis=1)
        small.append(
            lax.dot_general(ahead, wide, LAST, precision=HIGHEST, preferred_element_type=jnp.float32)
            + lax.dot_general(wide, back, LAST, precision=HIGHEST, preferred_element_type=jnp.float32)
        )
    small.append(jnp.zeros((ev, width - top), jnp.float32))
    packed = jnp.concatenate(small, axis=1)
    for a in range(nc):
        for t in range(terms):
            total = jnp.zeros((ev, width), jnp.float32)
            for k in range(slots):
                total += jnp.where(rows[0, t, 0, k] == a, 1.0, 0.0) * forward[t * slots + k]
            fpart[a, t] = total
        fpart[a, terms] = packed

    def fp(p):
        return remote(fpart.at[p], frecv.at[c], f_send.at[p], f_recv.at[c], r, p)

    each_col(lambda p: fp(p).start())
    frecv[c] = fpart[c]
    each_col(
        lambda p: remote(fpart.at[p], frecv.at[p], f_send.at[p], f_recv.at[p], r, p).wait_recv()
    )
    sums = frecv[0]
    for a in range(1, nc):
        sums += frecv[a]
    ssend[...] = sums[terms]
    srecv[r] = sums[terms]

    def sp(p):
        return remote(ssend, srecv.at[r], s_send.at[p], s_recv.at[r], p, c)

    each_row(lambda p: sp(p).start())

    app_ref[...] = sums[:terms] + mpart[r]

    @pl.loop(0, nr - 1 - r)
    def _(i):
        s = r + 1 + i
        remote(mpart.at[s], mrecv.at[s], m_send.at[s], m_recv.at[s], s, c).wait_recv()
        app_ref[...] += mrecv[s]

    each_row(lambda p: remote(ssend, srecv.at[p], s_send.at[p], s_recv.at[p], p, c).wait_recv())
    whole = srecv[0]
    for s in range(1, nr):
        whole += srecv[s]
    for t in range(terms):
        sub_ref[t] = whole[:, t * ev : (t + 1) * ev] * scale

    each_col(lambda p: rv(p).wait_send())
    each_col(lambda p: fp(p).wait_send())
    each_row(lambda p: sp(p).wait_send())

    @pl.loop(0, nr - 1 - r)
    def _(i):
        cv(nr - 1 - i).wait_send()

    @pl.loop(0, r)
    def _(b):
        mp(b).wait_send()


def flip(table):
    return jnp.swapaxes(table, 1, 2)


def shards(nr, nc, vectors, tile_vals, tile_rows, tile_cols, tile_counts, tile_diag):
    ev, width = vectors.shape
    terms, slots = tile_vals.shape[2], tile_vals.shape[3]
    f32 = jnp.float32
    scale = 1.0 / math.sqrt(width * nr * nc)
    vmem = pl.BlockSpec(memory_space=pltpu.VMEM)
    smem = pl.BlockSpec(memory_space=pltpu.SMEM)
    dma = pltpu.SemaphoreType.DMA
    return pl.pallas_call(
        functools.partial(kernel, nr, nc, scale),
        out_shape=(
            jax.ShapeDtypeStruct((terms, ev, width), f32),
            jax.ShapeDtypeStruct((terms, ev, ev), f32),
        ),
        in_specs=[vmem, pl.BlockSpec(memory_space=pl.ANY), smem, smem, smem, smem],
        out_specs=(vmem, vmem),
        scratch_shapes=[
            pltpu.VMEM(tile_vals.shape[2:], tile_vals.dtype),
            pltpu.VMEM((nc, ev, width), vectors.dtype),
            pltpu.VMEM((nr, ev, width), vectors.dtype),
            pltpu.VMEM((terms, slots, ev, width), f32),
            pltpu.VMEM((nr, terms, ev, width), f32),
            pltpu.VMEM((nr, terms, ev, width), f32),
            pltpu.VMEM((nc, terms + 1, ev, width), f32),
            pltpu.VMEM((nc, terms + 1, ev, width), f32),
            pltpu.VMEM((ev, width), f32),
            pltpu.VMEM((nr, ev, width), f32),
            dma,
            dma((nc,)), dma((nc,)), dma((nr,)), dma((nr,)), dma((nr,)), dma((nr,)),
            dma((nc,)), dma((nc,)), dma((nr,)), dma((nr,)),
        ],
        compiler_params=pltpu.CompilerParams(collective_id=0, has_side_effects=True),
    )(vectors, tile_vals, flip(tile_rows), flip(tile_cols), tile_counts, flip(tile_diag))


def solution(mesh):
    placed = (
        P(None, ("row", "col")),
        P("row", "col", None, None, None, None),
        P("row", "col", None, None),
        P("row", "col", None, None),
        P("row", "col", None),
        P("row", "col", None, None),
    )
    return jax.shard_map(
        functools.partial(shards, mesh.shape["row"], mesh.shape["col"]),
        mesh=mesh,
        in_specs=placed,
        out_specs=(P(None, None, ("row", "col")), P()),
        check_vma=False,
    )
```

time: 154 us -> 23.4 us (0.15)
  blocking collectives: 68 us -> 0 us
  waiting for transfers between devices: 52.6 us -> 0 us
  Pallas kernels: 0 us -> 20.6 us
  between operations: 14.2 us -> 0.65 us
  local copies, waits for them, and re-layouts: 7.96 us -> 1.92 us
  other arithmetic: 5.79 us -> 0 us
  matrix products: 4.7 us -> 0 us
    reduce_scatter x2 -> x0, waiting for transfers between devices: 52.6 us -> none  [the longest x1 52.6 us: shards(): lax.psum_scatter(jnp.stack(mirror_list), 'row', scatter_dimension=2, tile...]
    psum x1 -> x0, blocking collectives: 40.2 us -> none  [shards(): lax.psum(local_terms[term_idx], ('row', 'col'))]
    all_gather x2 -> x0, blocking collectives: 27.8 us -> none  [the longest x1 23.4 us: shards(): col_block = lax.all_gather(vectors, 'row', axis=1, tiled=True)]
    pallas_call x0 -> x1, Pallas kernels: none -> 20.6 us  [shards(): pl.pallas_call(functools.partial(kernel, nr, nc, scale), out_shape=(jax.S...]
    dot_general x13 -> x0, matrix products: 4.7 us -> none  [the longest x3 2.39 us: place_terms(): jnp.einsum('kij,ekj->eki', tiles_now, picked_cols, preferred_element_type...]
    gather x6 -> x0, local copies, waits for them, and re-layouts: 3.36 us -> none  [the longest x3 1.68 us: place_terms(): picked_rows = jnp.take(row_segs, rows_now, axis=1)]
    convert_element_type x3 -> x0, other arithmetic: 1.86 us -> none  [shards(): live_wt = (slot_ids < tile_counts[0, 0, term_idx]).astype(jnp.float32)]
    mul x1 -> x0, other arithmetic: 1.86 us -> none  [shards(): mirror_wt = live_wt * (1 - tile_diag[0, 0, term_idx]).astype(jnp.float32)]
  transfers between devices with their start and end apart: 2 -> 0, of which waited for: 1 -> 0; matrix products, arithmetic and copies ran while one was open for 4% -> 0% of each run, Pallas kernels for 0% -> 0%
where the time goes in v1:
time: 23.4 us; the launch traced here: 23.2 us
  Pallas kernels  20.6 us (88%)
  local copies, waits for them, and re-layouts  1.92 us (8%)
  between operations  0.65 us (3%)
    pallas_call x1, Pallas kernels, shards(): pl.pallas_call(functools.partial(kernel, nr, nc, scale), out_shape=(jax.S...  20.6 us
    unnamed x4, local copies, waits for them, and re-layouts  1.92 us

profile of v1, /device:TPU:0, one launch (start us, length us, event | category | flops | bytes accessed | tf_op | source)
XLA Modules:
  0.0 23.2 jit_solution(17051172311773791448)
XLA Ops:
  0.6 20.6 %shard_map.77 = (f32[3,8,128]{2,1,0:T(8,128)}, f32[3,8,8]{2,1,0:T(8,128)}) custom-call(bf16[8,128]{1,0:T(8,128)(2,1)} %v_ref.1, bf16[1,1,3,4,128,128]{5,4,3,2,1,0:T(8,128)(2,1)} %w_hbm.1, s32[1,3,1,4]{3,2,1,0:T(1,128)} %bitcast.3, s32[1,3,1,4]{3,2,1,0:T(1,128)} %bitcast.4, s32[1,1,3]{2,1,0:T(1,128)} %counts.1, s32[1,3,1,4]{3,2,1,0:T(1,128)} %bitcast.5), custom_call_target="tpu_custom_call" | custom-call | tf_op jit(solution)/shard_map/pallas_call | solution.py:193
  21.3 0.0 copy-start
  21.3 1.3 %copy.10 = f32[3,8,128]{2,1,0:T(8,128)} copy(f32[3,8,128]{2,1,0:T(8,128)} %get-tuple-element.4) | data formatting | bytes 24576
  22.6 0.0 copy-done
  22.6 0.6 %copy.11 = f32[3,8,8]{2,1,0:T(8,128)} copy(f32[3,8,8]{2,1,0:T(8,128)S(1)} %copy-done) | data formatting | bytes 1536
Async XLA Ops:
  21.3 1.3 %copy-start = (f32[3,8,8]{2,1,0:T(8,128)S(1)}, f32[3,8,8]{2,1,0:T(8,128)}, u32[]{:S(2)}) copy-start(f32[3,8,8]{2,1,0:T(8,128)} %get-tuple-element.5) | copy-start | bytes 2308

commit v2 on v1

--- a/solution.py
+++ b/solution.py
@@ -17,11 +17,13 @@
     nr, nc, scale,
     v_ref, w_hbm, rows, cols, counts, diag,
     app_ref, sub_ref,
-    w, rowv, colv, mterm, mpart, mrecv, fpart, frecv, ssend, srecv,
-    w_sem, rv_send, rv_recv, cv_send, cv_recv, m_send, m_recv, f_send, f_recv, s_send, s_recv,
+    w, rowv, colv, mterm, mpart, pair, msum, mrecv, fpart, frecv, ssend, srecv,
+    w_sem, rv_send, rv_recv, cv_send, cv_recv, p_send, p_recv, m_send, m_recv, f_send, f_recv, s_send, s_recv,
 ):
     r = lax.axis_index("row")
     c = lax.axis_index("col")
+    q = r // 2
+    half = lax.rem(r, 2)
     ev, width = v_ref.shape
     terms, slots = w.shape[0], w.shape[1]
     top = terms * ev
@@ -44,6 +46,14 @@
 
     w_copy = pltpu.make_async_copy(w_hbm.at[0, 0], w, w_sem)
     w_copy.start()
+
+    live = []
+    off = []
+    for t in range(terms):
+        for k in range(slots):
+            alive = k < counts[0, 0, t]
+            live.append(jnp.where(alive, 1.0, 0.0).astype(jnp.float32))
+            off.append(jnp.where(alive & (diag[0, t, 0, k] == 0), 1.0, 0.0).astype(jnp.float32))
 
     barrier = pltpu.get_barrier_semaphore()
     each_row(lambda p: pl.semaphore_signal(barrier, inc=1, device_id=(p, c), device_id_type=MESH))
@@ -73,32 +83,52 @@
     w_copy.wait()
     each_col(lambda p: remote(v_ref, rowv.at[p], rv_send.at[p], rv_recv.at[p], r, p).wait_recv())
 
-    live = []
-    off = []
     for t in range(terms):
         for k in range(slots):
-            alive = k < counts[0, 0, t]
-            live.append(jnp.where(alive, 1.0, 0.0).astype(jnp.float32))
-            off.append(jnp.where(alive & (diag[0, t, 0, k] == 0), 1.0, 0.0).astype(jnp.float32))
             mterm[t, k] = jnp.dot(
                 rowv[rows[0, t, 0, k]], w[t, k], preferred_element_type=jnp.float32
             )
 
-    @pl.loop(0, r + 1)
-    def _(b):
+    def place(side, j):
+        b = 2 * j + side
         for t in range(terms):
             total = jnp.zeros((ev, width), jnp.float32)
             for k in range(slots):
                 weight = jnp.where(cols[0, t, 0, k] == b, off[t * slots + k], 0.0)
                 total += weight * mterm[t, k]
-            mpart[b, t] = total
-
-    def mp(b):
-        return remote(mpart.at[b], mrecv.at[r], m_send.at[b], m_recv.at[r], b, c)
-
-    @pl.loop(0, r)
-    def _(b):
-        mp(b).start()
+            mpart[side, j, t] = total
+
+    def pp(j):
+        return remote(
+            mpart.at[1 - half, j], pair.at[j], p_send.at[j], p_recv.at[j], r + 1 - 2 * half, c
+        )
+
+    place(1 - half, 0)
+
+    @pl.loop(1, q + 1)
+    def _(j):
+        place(1 - half, j)
+        pp(j - 1).start()
+
+    pp(q).start()
+
+    @pl.loop(0, q + 1)
+    def _(j):
+        place(half, j)
+
+    def mp(j):
+        return remote(
+            msum.at[j], mrecv.at[q], m_send.at[j], m_recv.at[q], 2 * j + half, c
+        )
+
+    pp(0).wait_recv()
+    msum[0] = mpart[half, 0] + pair[0]
+
+    @pl.loop(1, q + 1)
+    def _(j):
+        pp(j).wait_recv()
+        msum[j] = mpart[half, j] + pair[j]
+        mp(j - 1).start()
 
     @pl.loop(0, r)
     def _(b):
@@ -150,12 +180,13 @@
 
     each_row(lambda p: sp(p).start())
 
-    app_ref[...] = sums[:terms] + mpart[r]
-
-    @pl.loop(0, nr - 1 - r)
-    def _(i):
-        s = r + 1 + i
-        remote(mpart.at[s], mrecv.at[s], m_send.at[s], m_recv.at[s], s, c).wait_recv()
+    app_ref[...] = sums[:terms] + msum[q]
+
+    @pl.loop(q + 1, nr // 2)
+    def _(s):
+        remote(
+            msum.at[s], mrecv.at[s], m_send.at[s], m_recv.at[s], 2 * s + half, c
+        ).wait_recv()
         app_ref[...] += mrecv[s]
 
     each_row(lambda p: remote(ssend, srecv.at[p], s_send.at[p], s_recv.at[p], p, c).wait_recv())
@@ -173,9 +204,13 @@
     def _(i):
         cv(nr - 1 - i).wait_send()
 
-    @pl.loop(0, r)
-    def _(b):
-        mp(b).wait_send()
+    @pl.loop(0, q + 1)
+    def _(j):
+        pp(j).wait_send()
+
+    @pl.loop(0, q)
+    def _(j):
+        mp(j).wait_send()
 
 
 def flip(table):
@@ -203,14 +238,17 @@
             pltpu.VMEM((nc, ev, width), vectors.dtype),
             pltpu.VMEM((nr, ev, width), vectors.dtype),
             pltpu.VMEM((terms, slots, ev, width), f32),
-            pltpu.VMEM((nr, terms, ev, width), f32),
-            pltpu.VMEM((nr, terms, ev, width), f32),
+            pltpu.VMEM((2, nr // 2, terms, ev, width), f32),
+            pltpu.VMEM((nr // 2, terms, ev, width), f32),
+            pltpu.VMEM((nr // 2, terms, ev, width), f32),
+            pltpu.VMEM((nr // 2, terms, ev, width), f32),
             pltpu.VMEM((nc, terms + 1, ev, width), f32),
             pltpu.VMEM((nc, terms + 1, ev, width), f32),
             pltpu.VMEM((ev, width), f32),
             pltpu.VMEM((nr, ev, width), f32),
             dma,
-            dma((nc,)), dma((nc,)), dma((nr,)), dma((nr,)), dma((nr,)), dma((nr,)),
+            dma((nc,)), dma((nc,)), dma((nr,)), dma((nr,)),
+            dma((nr // 2,)), dma((nr // 2,)), dma((nr // 2,)), dma((nr // 2,)),
             dma((nc,)), dma((nc,)), dma((nr,)), dma((nr,)),
         ],
         compiler_params=pltpu.CompilerParams(collective_id=0, has_side_effects=True),

time: 23.4 us -> 23.4 us (level)
  no operation moved by 1% of the time
where the time goes in v2:
time: 23.4 us; the launch traced here: 23.2 us
  Pallas kernels  20.7 us (88%)
  local copies, waits for them, and re-layouts  1.92 us (8%)
  between operations  0.65 us (3%)
    pallas_call x1, Pallas kernels, shards(): pl.pallas_call(functools.partial(kernel, nr, nc, scale), out_shape=(jax.S...  20.7 us
    unnamed x4, local copies, waits for them, and re-layouts  1.92 us

profile of v2, /device:TPU:0, one launch (start us, length us, event | category | flops | bytes accessed | tf_op | source)
XLA Modules:
  0.0 23.2 jit_solution(17229905748098555670)
XLA Ops:
  0.6 20.7 %shard_map.77 = (f32[3,8,128]{2,1,0:T(8,128)}, f32[3,8,8]{2,1,0:T(8,128)}) custom-call(bf16[8,128]{1,0:T(8,128)(2,1)} %v_ref.1, bf16[1,1,3,4,128,128]{5,4,3,2,1,0:T(8,128)(2,1)} %w_hbm.1, s32[1,3,1,4]{3,2,1,0:T(1,128)} %bitcast.3, s32[1,3,1,4]{3,2,1,0:T(1,128)} %bitcast.4, s32[1,1,3]{2,1,0:T(1,128)} %counts.1, s32[1,3,1,4]{3,2,1,0:T(1,128)} %bitcast.5), custom_call_target="tpu_custom_call" | custom-call | tf_op jit(solution)/shard_map/pallas_call | solution.py:228
  21.3 0.0 copy-start
  21.3 1.3 %copy.10 = f32[3,8,128]{2,1,0:T(8,128)} copy(f32[3,8,128]{2,1,0:T(8,128)} %get-tuple-element.4) | data formatting | bytes 24576
  22.6 0.0 copy-done
  22.6 0.6 %copy.11 = f32[3,8,8]{2,1,0:T(8,128)} copy(f32[3,8,8]{2,1,0:T(8,128)S(1)} %copy-done) | data formatting | bytes 1536
Async XLA Ops:
  21.3 1.3 %copy-start = (f32[3,8,8]{2,1,0:T(8,128)S(1)}, f32[3,8,8]{2,1,0:T(8,128)}, u32[]{:S(2)}) copy-start(f32[3,8,8]{2,1,0:T(8,128)} %get-tuple-element.5) | copy-start | bytes 2308

commit v3 on v2

v3 whole, which is shorter than its diff:
```python
import functools
import math

import jax
import jax.numpy as jnp
from jax import lax
from jax.experimental import pallas as pl
from jax.experimental.pallas import tpu as pltpu
from jax.sharding import PartitionSpec as P

MESH = pl.DeviceIdType.MESH
LAST = (((1,), (1,)), ((), ()))


def kernel(
    nr, nc, scale,
    v_hbm, w_hbm, rows_hbm, cols_hbm, counts_hbm, diag_hbm,
    app_ref, sub_ref,
    v_ref, rows, cols, counts, diag,
    w, rowv, colv, mterm, ahead, back, mpart, pair, msum, mrecv, fpart, frecv, yrecv, ssend, srecv,
    in_sem, w_sem, rv_send, rv_recv, cv_send, cv_recv, p_send, p_recv, m_send, m_recv,
    f_send, f_recv, y_send, y_recv, s_send, s_recv,
):
    r = lax.axis_index("row")
    c = lax.axis_index("col")
    q = r // 2
    half = lax.rem(r, 2)
    ev, width = v_ref.shape
    terms, slots = w.shape[0], w.shape[1]
    top = terms * ev

    def remote(src, dst, send, recv, row, col):
        return pltpu.make_async_remote_copy(
            src_ref=src, dst_ref=dst, send_sem=send, recv_sem=recv,
            device_id=(row, col), device_id_type=MESH,
        )

    def each_row(fn):
        @pl.loop(1, nr)
        def _(d):
            fn(lax.rem(r + d, nr))

    def each_col(fn):
        @pl.loop(1, nc)
        def _(d):
            fn(lax.rem(c + d, nc))

    barrier = pltpu.get_barrier_semaphore()
    each_row(lambda p: pl.semaphore_signal(barrier, inc=1, device_id=(p, c), device_id_type=MESH))
    each_col(lambda p: pl.semaphore_signal(barrier, inc=1, device_id=(r, p), device_id_type=MESH))

    small_in = [
        pltpu.make_async_copy(src, dst, in_sem.at[i])
        for i, (src, dst) in enumerate(
            [(v_hbm, v_ref), (rows_hbm, rows), (cols_hbm, cols), (counts_hbm, counts), (diag_hbm, diag)]
        )
    ]
    for copy in small_in:
        copy.start()
    w_copy = pltpu.make_async_copy(w_hbm.at[0, 0], w, w_sem)
    w_copy.start()
    zero = jnp.zeros((ev, width), v_ref.dtype)

    @pl.loop(r + 1, nr)
    def _(b):
        colv[b] = zero

    for copy in small_in:
        copy.wait()
    own = v_ref[...]
    rowv[c] = own
    colv[r] = own
    live = []
    off = []
    for t in range(terms):
        for k in range(slots):
            alive = k < counts[0, 0, t]
            live.append(jnp.where(alive, 1.0, 0.0).astype(jnp.float32))
            off.append(jnp.where(alive & (diag[0, t, 0, k] == 0), 1.0, 0.0).astype(jnp.float32))
    pl.semaphore_wait(barrier, nr - 1 + nc - 1)

    def rv(p):
        return remote(v_ref, rowv.at[c], rv_send.at[p], rv_recv.at[c], r, p)

    def cv(p):
        return remote(v_ref, colv.at[r], cv_send.at[p], cv_recv.at[r], p, c)

    each_col(lambda p: rv(p).start())

    @pl.loop(0, nr - 1 - r)
    def _(i):
        cv(nr - 1 - i).start()

    w_copy.wait()
    each_col(lambda p: remote(v_ref, rowv.at[p], rv_send.at[p], rv_recv.at[p], r, p).wait_recv())

    for t in range(terms):
        for k in range(slots):
            mterm[t, k] = jnp.dot(
                rowv[rows[0, t, 0, k]], w[t, k], preferred_element_type=jnp.float32
            )

    def place(side, j):
        b = 2 * j + side
        for t in range(terms):
            total = jnp.zeros((ev, width), jnp.float32)
            for k in range(slots):
                weight = jnp.where(cols[0, t, 0, k] == b, off[t * slots + k], 0.0)
                total += weight * mterm[t, k]
            mpart[side, j, t] = total

    def pp(j):
        return remote(
            mpart.at[1 - half, j], pair.at[j], p_send.at[j], p_recv.at[j], r + 1 - 2 * half, c
        )

    place(1 - half, 0)

    @pl.loop(1, q + 1)
    def _(j):
        place(1 - half, j)
        pp(j - 1).start()

    pp(q).start()

    @pl.loop(0, q + 1)
    def _(j):
        place(half, j)

    def parts(value):
        high = value.astype(jnp.bfloat16)
        rest = value - high.astype(jnp.float32)
        middle = rest.astype(jnp.bfloat16)
        low = (rest - middle.astype(jnp.float32)).astype(jnp.bfloat16)
        return jnp.concatenate([high, middle, low], axis=0)

    for t in range(terms):
        for k in range(slots):
            lanes = pl.ds(k * width, width)
            split = parts(mterm[t, k])
            ahead[t, :, lanes] = split * live[t * slots + k].astype(jnp.bfloat16)
            back[t, :, lanes] = split * off[t * slots + k].astype(jnp.bfloat16)

    @pl.loop(0, r)
    def _(b):
        remote(v_ref, colv.at[b], cv_send.at[b], cv_recv.at[b], b, c).wait_recv()

    small = []
    for t in range(terms):
        wide = jnp.concatenate(
            [colv[jnp.minimum(cols[0, t, 0, k], r)] for k in range(slots)], axis=1
        )
        one = lax.dot_general(ahead[t], wide, LAST, preferred_element_type=jnp.float32)
        two = lax.dot_general(wide, back[t], LAST, preferred_element_type=jnp.float32)
        small.append(
            (one[2 * ev :] + one[ev : 2 * ev]) + one[:ev]
            + ((two[:, 2 * ev :] + two[:, ev : 2 * ev]) + two[:, :ev])
        )
    small.append(jnp.zeros((ev, width - top), jnp.float32))
    packed = jnp.concatenate(small, axis=1)

    per = width // top
    lines = -(-ev // per)
    line = lax.broadcasted_iota(jnp.int32, (ev, width), 0)
    group = lax.broadcasted_iota(jnp.int32, (ev, width), 1) // top
    spread = packed
    for g in range(1, per):
        spread += pltpu.roll(packed, g * top, 1)
    for n in range(lines):
        picked = jnp.where(line == group + n * per, jnp.where(group < per, spread, 0.0), 0.0)
        ssend[0, n] = jnp.sum(picked, axis=0)

    def yp(p):
        return remote(ssend.at[0], yrecv.at[c], y_send.at[p], y_recv.at[c], r, p)

    each_col(lambda p: yp(p).start())
    yrecv[c] = ssend[0]

    for t in range(terms):
        totals = [jnp.zeros((ev, width), jnp.float32) for _ in range(nc)]
        for k in range(slots):
            seen = colv[jnp.minimum(cols[0, t, 0, k], r)]
            moved = lax.dot_general(seen, w[t, k], LAST, preferred_element_type=jnp.float32)
            for a in range(nc):
                weight = jnp.where(rows[0, t, 0, k] == a, live[t * slots + k], 0.0)
                totals[a] += weight * moved
        for a in range(nc):
            fpart[a, t] = totals[a]

    def fp(p):
        return remote(fpart.at[p], frecv.at[c], f_send.at[p], f_recv.at[c], r, p)

    each_col(lambda p: fp(p).start())
    frecv[c] = fpart[c]

    def mp(j):
        return remote(
            msum.at[j], mrecv.at[q], m_send.at[j], m_recv.at[q], 2 * j + half, c
        )

    pp(0).wait_recv()
    msum[0] = mpart[half, 0] + pair[0]

    @pl.loop(1, q + 1)
    def _(j):
        pp(j).wait_recv()
        msum[j] = mpart[half, j] + pair[j]
        mp(j - 1).start()

    each_col(
        lambda p: remote(ssend.at[0], yrecv.at[p], y_send.at[p], y_recv.at[p], r, p).wait_recv()
    )
    level = yrecv[0]
    for a in range(1, nc):
        level += yrecv[a]
    ssend[1] = level
    srecv[r] = level

    def sp(p):
        return remote(ssend.at[1], srecv.at[r], s_send.at[p], s_recv.at[r], p, c)

    each_row(lambda p: sp(p).start())

    each_col(
        lambda p: remote(fpart.at[p], frecv.at[p], f_send.at[p], f_recv.at[p], r, p).wait_recv()
    )
    sums = frecv[0]
    for a in range(1, nc):
        sums += frecv[a]
    app_ref[...] = sums + msum[q]

    @pl.loop(q + 1, nr // 2)
    def _(s):
        remote(
            msum.at[s], mrecv.at[s], m_send.at[s], m_recv.at[s], 2 * s + half, c
        ).wait_recv()
        app_ref[...] += mrecv[s]

    each_row(
        lambda p: remote(ssend.at[1], srecv.at[p], s_send.at[p], s_recv.at[p], p, c).wait_recv()
    )
    whole = srecv[0]
    for s in range(1, nr):
        whole += srecv[s]
    picked = jnp.zeros((ev, width), jnp.float32)
    for n in range(lines):
        picked += jnp.where(
            line == group + n * per,
            jnp.where(group < per, jnp.broadcast_to(whole[n : n + 1], (ev, width)), 0.0),
            0.0,
        )
    spread = picked
    for g in range(1, per):
        spread += pltpu.roll(picked, width - g * top, 1)
    for t in range(terms):
        sub_ref[t] = spread[:, t * ev : (t + 1) * ev] * scale

    each_col(lambda p: yp(p).wait_send())
    each_col(lambda p: rv(p).wait_send())
    each_col(lambda p: fp(p).wait_send())
    each_row(lambda p: sp(p).wait_send())

    @pl.loop(0, nr - 1 - r)
    def _(i):
        cv(nr - 1 - i).wait_send()

    @pl.loop(0, q + 1)
    def _(j):
        pp(j).wait_send()

    @pl.loop(0, q)
    def _(j):
        mp(j).wait_send()


def flip(table):
    return jnp.swapaxes(table, 1, 2)


def shards(nr, nc, vectors, tile_vals, tile_rows, tile_cols, tile_counts, tile_diag):
    ev, width = vectors.shape
    terms, slots = tile_vals.shape[2], tile_vals.shape[3]
    f32 = jnp.float32
    scale = 1.0 / math.sqrt(width * nr * nc)
    vmem = pl.BlockSpec(memory_space=pltpu.VMEM)
    top = terms * ev
    lines = -(-ev // (width // top))
    table = pltpu.SMEM((1, terms, 1, slots), jnp.int32)
    dma = pltpu.SemaphoreType.DMA
    return pl.pallas_call(
        functools.partial(kernel, nr, nc, scale),
        out_shape=(
            jax.ShapeDtypeStruct((terms, ev, width), f32),
            jax.ShapeDtypeStruct((terms, ev, ev), f32),
        ),
        in_specs=[pl.BlockSpec(memory_space=pl.ANY)] * 6,
        out_specs=(vmem, vmem),
        scratch_shapes=[
            pltpu.VMEM(vectors.shape, vectors.dtype),
            table, table, pltpu.SMEM(tile_counts.shape, jnp.int32), table,
            pltpu.VMEM(tile_vals.shape[2:], tile_vals.dtype),
            pltpu.VMEM((nc, ev, width), vectors.dtype),
            pltpu.VMEM((nr, ev, width), vectors.dtype),
            pltpu.VMEM((terms, slots, ev, width), f32),
            pltpu.VMEM((terms, 3 * ev, slots * width), jnp.bfloat16),
            pltpu.VMEM((terms, 3 * ev, slots * width), jnp.bfloat16),
            pltpu.VMEM((2, nr // 2, terms, ev, width), f32),
            pltpu.VMEM((nr // 2, terms, ev, width), f32),
            pltpu.VMEM((nr // 2, terms, ev, width), f32),
            pltpu.VMEM((nr // 2, terms, ev, width), f32),
            pltpu.VMEM((nc, terms, ev, width), f32),
            pltpu.VMEM((nc, terms, ev, width), f32),
            pltpu.VMEM((nc, lines, width), f32),
            pltpu.VMEM((2, lines, width), f32),
            pltpu.VMEM((nr, lines, width), f32),
            dma((5,)), dma,
            dma((nc,)), dma((nc,)), dma((nr,)), dma((nr,)),
            dma((nr // 2,)), dma((nr // 2,)), dma((nr // 2,)), dma((nr // 2,)),
            dma((nc,)), dma((nc,)), dma((nc,)), dma((nc,)), dma((nr,)), dma((nr,)),
        ],
        compiler_params=pltpu.CompilerParams(collective_id=0, has_side_effects=True),
    )(vectors, tile_vals, flip(tile_rows), flip(tile_cols), tile_counts, flip(tile_diag))


def solution(mesh):
    placed = (
        P(None, ("row", "col")),
        P("row", "col", None, None, None, None),
        P("row", "col", None, None),
        P("row", "col", None, None),
        P("row", "col", None),
        P("row", "col", None, None),
    )
    return jax.shard_map(
        functools.partial(shards, mesh.shape["row"], mesh.shape["col"]),
        mesh=mesh,
        in_specs=placed,
        out_specs=(P(None, None, ("row", "col")), P()),
        check_vma=False,
    )
```

time: 23.4 us -> 22.3 us (0.953)
  Pallas kernels: 20.7 us -> 19.5 us
    pallas_call x1, Pallas kernels: 20.7 us -> 19.5 us  [shards(): pl.pallas_call(functools.partial(kernel, nr, nc, scale), out_shape=(jax.S...]
where the time goes in v3:
time: 22.3 us; the launch traced here: 22.1 us
  Pallas kernels  19.5 us (87%)
  local copies, waits for them, and re-layouts  1.92 us (9%)
  between operations  0.65 us (3%)
    pallas_call x1, Pallas kernels, shards(): pl.pallas_call(functools.partial(kernel, nr, nc, scale), out_shape=(jax.S...  19.5 us
    unnamed x4, local copies, waits for them, and re-layouts  1.92 us

profile of v3, /device:TPU:0, one launch (start us, length us, event | category | flops | bytes accessed | tf_op | source)
XLA Modules:
  0.0 22.1 jit_solution(10090519021922626171)
XLA Ops:
  0.6 19.5 %shard_map.77 = (f32[3,8,128]{2,1,0:T(8,128)}, f32[3,8,8]{2,1,0:T(8,128)}) custom-call(bf16[8,128]{1,0:T(8,128)(2,1)} %v_hbm.1, bf16[1,1,3,4,128,128]{5,4,3,2,1,0:T(8,128)(2,1)} %w_hbm.1, s32[1,3,1,4]{3,2,1,0:T(1,128)} %bitcast.3, s32[1,3,1,4]{3,2,1,0:T(1,128)} %bitcast.4, s32[1,1,3]{2,1,0:T(1,128)} %counts_hbm.1, s32[1,3,1,4]{3,2,1,0:T(1,128)} %bitcast.5), custom_call_target="tpu_custom_call" | custom-call | tf_op jit(solution)/shard_map/pallas_call | solution.py:290
  20.1 0.0 copy-start
  20.2 1.3 %copy.10 = f32[3,8,128]{2,1,0:T(8,128)} copy(f32[3,8,128]{2,1,0:T(8,128)} %get-tuple-element.4) | data formatting | bytes 24576
  21.5 0.0 copy-done
  21.5 0.6 %copy.11 = f32[3,8,8]{2,1,0:T(8,128)} copy(f32[3,8,8]{2,1,0:T(8,128)S(1)} %copy-done) | data formatting | bytes 1536
Async XLA Ops:
  20.1 1.3 %copy-start = (f32[3,8,8]{2,1,0:T(8,128)S(1)}, f32[3,8,8]{2,1,0:T(8,128)}, u32[]{:S(2)}) copy-start(f32[3,8,8]{2,1,0:T(8,128)} %get-tuple-element.5) | copy-start | bytes 2308

commit v4 on v3

--- a/solution.py
+++ b/solution.py
@@ -8,6 +8,7 @@
 from jax.experimental.pallas import tpu as pltpu
 from jax.sharding import PartitionSpec as P
 
+LIMIT = 16 * 2**20
 MESH = pl.DeviceIdType.MESH
 LAST = (((1,), (1,)), ((), ()))
 
@@ -17,9 +18,9 @@
     v_hbm, w_hbm, rows_hbm, cols_hbm, counts_hbm, diag_hbm,
     app_ref, sub_ref,
     v_ref, rows, cols, counts, diag,
-    w, rowv, colv, mterm, ahead, back, mpart, pair, msum, mrecv, fpart, frecv, yrecv, ssend, srecv,
+    w, rowv, colv, mterm, ahead, back, mpart, pair, msum, mrecv, fpart, frecv, ssend, srecv,
     in_sem, w_sem, rv_send, rv_recv, cv_send, cv_recv, p_send, p_recv, m_send, m_recv,
-    f_send, f_recv, y_send, y_recv, s_send, s_recv,
+    f_send, f_recv, s_send, s_recv,
 ):
     r = lax.axis_index("row")
     c = lax.axis_index("col")
@@ -168,13 +169,22 @@
         spread += pltpu.roll(packed, g * top, 1)
     for n in range(lines):
         picked = jnp.where(line == group + n * per, jnp.where(group < per, spread, 0.0), 0.0)
-        ssend[0, n] = jnp.sum(picked, axis=0)
-
-    def yp(p):
-        return remote(ssend.at[0], yrecv.at[c], y_send.at[p], y_recv.at[c], r, p)
-
-    each_col(lambda p: yp(p).start())
-    yrecv[c] = ssend[0]
+        ssend[n] = jnp.sum(picked, axis=0)
+
+    me = r * nc + c
+
+    def sp(p):
+        return remote(
+            ssend, srecv.at[me], s_send.at[p], s_recv.at[me], p // nc, lax.rem(p, nc)
+        )
+
+    def each_device(fn):
+        @pl.loop(1, nr * nc)
+        def _(d):
+            fn(lax.rem(me + d, nr * nc))
+
+    each_device(lambda p: sp(p).start())
+    srecv[me] = ssend[...]
 
     for t in range(terms):
         totals = [jnp.zeros((ev, width), jnp.float32) for _ in range(nc)]
@@ -208,20 +218,6 @@
         mp(j - 1).start()
 
     each_col(
-        lambda p: remote(ssend.at[0], yrecv.at[p], y_send.at[p], y_recv.at[p], r, p).wait_recv()
-    )
-    level = yrecv[0]
-    for a in range(1, nc):
-        level += yrecv[a]
-    ssend[1] = level
-    srecv[r] = level
-
-    def sp(p):
-        return remote(ssend.at[1], srecv.at[r], s_send.at[p], s_recv.at[r], p, c)
-
-    each_row(lambda p: sp(p).start())
-
-    each_col(
         lambda p: remote(fpart.at[p], frecv.at[p], f_send.at[p], f_recv.at[p], r, p).wait_recv()
     )
     sums = frecv[0]
@@ -236,11 +232,13 @@
         ).wait_recv()
         app_ref[...] += mrecv[s]
 
-    each_row(
-        lambda p: remote(ssend.at[1], srecv.at[p], s_send.at[p], s_recv.at[p], p, c).wait_recv()
+    each_device(
+        lambda p: remote(
+            ssend, srecv.at[p], s_send.at[p], s_recv.at[p], p // nc, lax.rem(p, nc)
+        ).wait_recv()
     )
     whole = srecv[0]
-    for s in range(1, nr):
+    for s in range(1, nr * nc):
         whole += srecv[s]
     picked = jnp.zeros((ev, width), jnp.float32)
     for n in range(lines):
@@ -255,10 +253,9 @@
     for t in range(terms):
         sub_ref[t] = spread[:, t * ev : (t + 1) * ev] * scale
 
-    each_col(lambda p: yp(p).wait_send())
     each_col(lambda p: rv(p).wait_send())
     each_col(lambda p: fp(p).wait_send())
-    each_row(lambda p: sp(p).wait_send())
+    each_device(lambda p: sp(p).wait_send())
 
     @pl.loop(0, nr - 1 - r)
     def _(i):
@@ -283,17 +280,18 @@
     f32 = jnp.float32
     scale = 1.0 / math.sqrt(width * nr * nc)
     vmem = pl.BlockSpec(memory_space=pltpu.VMEM)
+    hbm = pl.BlockSpec(memory_space=pltpu.MemorySpace.HBM)
     top = terms * ev
     lines = -(-ev // (width // top))
     table = pltpu.SMEM((1, terms, 1, slots), jnp.int32)
     dma = pltpu.SemaphoreType.DMA
-    return pl.pallas_call(
+    return finish(*pl.pallas_call(
         functools.partial(kernel, nr, nc, scale),
         out_shape=(
             jax.ShapeDtypeStruct((terms, ev, width), f32),
             jax.ShapeDtypeStruct((terms, ev, ev), f32),
         ),
-        in_specs=[pl.BlockSpec(memory_space=pl.ANY)] * 6,
+        in_specs=[hbm] * 6,
         out_specs=(vmem, vmem),
         scratch_shapes=[
             pltpu.VMEM(vectors.shape, vectors.dtype),
@@ -310,16 +308,37 @@
             pltpu.VMEM((nr // 2, terms, ev, width), f32),
             pltpu.VMEM((nc, terms, ev, width), f32),
             pltpu.VMEM((nc, terms, ev, width), f32),
-            pltpu.VMEM((nc, lines, width), f32),
-            pltpu.VMEM((2, lines, width), f32),
-            pltpu.VMEM((nr, lines, width), f32),
+            pltpu.VMEM((lines, width), f32),
+            pltpu.VMEM((nr * nc, lines, width), f32),
             dma((5,)), dma,
             dma((nc,)), dma((nc,)), dma((nr,)), dma((nr,)),
             dma((nr // 2,)), dma((nr // 2,)), dma((nr // 2,)), dma((nr // 2,)),
-            dma((nc,)), dma((nc,)), dma((nc,)), dma((nc,)), dma((nr,)), dma((nr,)),
+            dma((nc,)), dma((nc,)), dma((nr * nc,)), dma((nr * nc,)),
         ],
-        compiler_params=pltpu.CompilerParams(collective_id=0, has_side_effects=True),
-    )(vectors, tile_vals, flip(tile_rows), flip(tile_cols), tile_counts, flip(tile_diag))
+        compiler_params=pltpu.CompilerParams(collective_id=0, has_side_effects=True, vmem_limit_bytes=LIMIT),
+    )(vectors, tile_vals, flip(tile_rows), flip(tile_cols), tile_counts, flip(tile_diag)))
+
+
+def finish(applied, subspace):
+    def body(a_ref, b_ref, c_ref, d_ref, sem):
+        one = pltpu.make_async_copy(a_ref, c_ref, sem.at[0])
+        two = pltpu.make_async_copy(b_ref, d_ref, sem.at[1])
+        one.start()
+        two.start()
+        one.wait()
+        two.wait()
+
+    return pl.pallas_call(
+        body,
+        out_shape=(
+            jax.ShapeDtypeStruct(applied.shape, applied.dtype),
+            jax.ShapeDtypeStruct(subspace.shape, subspace.dtype),
+        ),
+        in_specs=[pl.BlockSpec(memory_space=pltpu.VMEM)] * 2,
+        out_specs=(pl.BlockSpec(memory_space=pltpu.MemorySpace.HBM),) * 2,
+        scratch_shapes=[pltpu.SemaphoreType.DMA((2,))],
+        compiler_params=pltpu.CompilerParams(vmem_limit_bytes=LIMIT),
+    )(applied, subspace)
 
 
 def solution(mesh):

time: 22.3 us -> 21.4 us (0.960)
  Pallas kernels: 19.5 us -> 18.2 us
  local copies, waits for them, and re-layouts: 1.92 us -> 2.37 us
    pallas_call x1, Pallas kernels: 19.5 us -> 17.6 us  [shards(): pl.pallas_call(functools.partial(kernel, nr, nc, scale), out_shape=(jax.S...]
    pallas_call x0 -> x1, Pallas kernels: none -> 0.62 us  [finish(): pl.pallas_call(body, out_shape=(jax.ShapeDtypeStruct(applied.shape, appli...]
    unnamed x4 -> x12, local copies, waits for them, and re-layouts: 1.92 us -> 2.37 us
where the time goes in v4:
time: 21.4 us; the launch traced here: 21.2 us
  Pallas kernels  18.2 us (85%)
  local copies, waits for them, and re-layouts  2.37 us (11%)
  between operations  0.68 us (3%)
    pallas_call x1, Pallas kernels, shards(): pl.pallas_call(functools.partial(kernel, nr, nc, scale), out_shape=(jax.S...  17.6 us
    unnamed x12, local copies, waits for them, and re-layouts  2.37 us
    pallas_call x1, Pallas kernels, finish(): pl.pallas_call(body, out_shape=(jax.ShapeDtypeStruct(applied.shape, appli...  0.62 us

profile of v4, /device:TPU:0, one launch (start us, length us, event | category | flops | bytes accessed | tf_op | source)
XLA Modules:
  0.0 21.2 jit_solution(5562284562553818420)
XLA Ops:
  0.6 0.0 copy-start.3
  0.6 0.0 copy-start.5
  0.7 0.0 copy-start.1
  0.7 0.0 copy-start.2
  0.7 0.6 %copy-done.3 = s32[1,1,3,4]{3,1,2,0:T(1,128)S(1)} copy-done((s32[1,1,3,4]{3,1,2,0:T(1,128)S(1)}, s32[1,1,3,4]{3,1,2,0:T(1,128)}, u32[]{:S(2)}) %copy-start.3) | copy-done | bytes 72
  1.3 0.0 copy-done.5
  1.3 0.0 copy-done.1
  1.3 0.0 copy-done.2
  1.4 0.0 copy-start
  1.4 1.0 %copy-done = bf16[1,1,3,4,128,128]{5,4,3,2,1,0:T(8,128)(2,1)S(1)} copy-done((bf16[1,1,3,4,128,128]{5,4,3,2,1,0:T(8,128)(2,1)S(1)}, bf16[1,1,3,4,128,128]{5,4,3,2,1,0:T(8,128)(2,1)}, u32[]{:S(2)}) %copy-start) | copy-done | bytes 393240
  2.4 0.0 copy-start.4
  2.4 0.7 %copy-done.4 = s32[1,1,3,4]{3,1,2,0:T(1,128)S(1)} copy-done((s32[1,1,3,4]{3,1,2,0:T(1,128)S(1)}, s32[1,1,3,4]{3,1,2,0:T(1,128)}, u32[]{:S(2)}) %copy-start.4) | copy-done | bytes 72
  3.0 17.6 %shard_map.77 = (f32[3,8,128]{2,1,0:T(8,128)S(1)}, f32[3,8,8]{2,1,0:T(8,128)S(1)}) custom-call(bf16[8,128]{1,0:T(8,128)(2,1)S(1)} %copy-done.1, bf16[1,1,3,4,128,128]{5,4,3,2,1,0:T(8,128)(2,1)S(1)} %copy-done, s32[1,3,1,4]{3,2,1,0:T(1,128)S(1)} %bitcast.3, s32[1,3,1,4]{3,2,1,0:T(1,128)S(1)} %bitcast.4, s32[1,1,3]{2,1,0:T(1,128)S(1)} %copy-done.5, ...), custom_call_target="tpu_custom_call" | custom-call | tf_op jit(solution)/shard_map/pallas_call | solution.py:288
  20.6 0.6 %shard_map.78 = (f32[3,8,128]{2,1,0:T(8,128)}, f32[3,8,8]{2,1,0:T(8,128)}) custom-call(f32[3,8,128]{2,1,0:T(8,128)S(1)} %get-tuple-element.4.a_ref, f32[3,8,8]{2,1,0:T(8,128)S(1)} %get-tuple-element.5.b_ref), custom_call_target="tpu_custom_call" | custom-call | tf_op jit(solution)/shard_map/pallas_call | solution.py:331
Async XLA Ops:
  0.6 0.7 %copy-start.3 = (s32[1,1,3,4]{3,1,2,0:T(1,128)S(1)}, s32[1,1,3,4]{3,1,2,0:T(1,128)}, u32[]{:S(2)}) copy-start(s32[1,1,3,4]{3,1,2,0:T(1,128)} %param.9) | copy-start | bytes 148
  0.6 0.7 %copy-start.5 = (s32[1,1,3]{2,1,0:T(1,128)S(1)}, s32[1,1,3]{2,1,0:T(1,128)}, u32[]{:S(2)}) copy-start(s32[1,1,3]{2,1,0:T(1,128)} %counts_hbm.1) | copy-start | bytes 40
  0.7 0.7 %copy-start.1 = (bf16[8,128]{1,0:T(8,128)(2,1)S(1)}, bf16[8,128]{1,0:T(8,128)(2,1)}, u32[]{:S(2)}) copy-start(bf16[8,128]{1,0:T(8,128)(2,1)} %v_hbm.1) | copy-start | bytes 6148
  0.7 0.7 %copy-start.2 = (s32[1,1,3,4]{3,1,2,0:T(1,128)S(1)}, s32[1,1,3,4]{3,1,2,0:T(1,128)}, u32[]{:S(2)}) copy-start(s32[1,1,3,4]{3,1,2,0:T(1,128)} %param.8) | copy-start | bytes 148
  1.4 1.0 %copy-start = (bf16[1,1,3,4,128,128]{5,4,3,2,1,0:T(8,128)(2,1)S(1)}, bf16[1,1,3,4,128,128]{5,4,3,2,1,0:T(8,128)(2,1)}, u32[]{:S(2)}) copy-start(bf16[1,1,3,4,128,128]{5,4,3,2,1,0:T(8,128)(2,1)} %w_hbm.1) | copy-start | bytes 1179652
  2.4 0.7 %copy-start.4 = (s32[1,1,3,4]{3,1,2,0:T(1,128)S(1)}, s32[1,1,3,4]{3,1,2,0:T(1,128)}, u32[]{:S(2)}) copy-start(s32[1,1,3,4]{3,1,2,0:T(1,128)} %param.11) | copy-start | bytes 148

commit v5 on v4

--- a/solution.py
+++ b/solution.py
@@ -8,7 +8,6 @@
 from jax.experimental.pallas import tpu as pltpu
 from jax.sharding import PartitionSpec as P
 
-LIMIT = 16 * 2**20
 MESH = pl.DeviceIdType.MESH
 LAST = (((1,), (1,)), ((), ()))
 
@@ -288,8 +287,8 @@
     return finish(*pl.pallas_call(
         functools.partial(kernel, nr, nc, scale),
         out_shape=(
-            jax.ShapeDtypeStruct((terms, ev, width), f32),
-            jax.ShapeDtypeStruct((terms, ev, ev), f32),
+            pltpu.VMEM((terms, ev, width), f32),
+            pltpu.VMEM((terms, ev, ev), f32),
         ),
         in_specs=[hbm] * 6,
         out_specs=(vmem, vmem),
@@ -315,7 +314,7 @@
             dma((nr // 2,)), dma((nr // 2,)), dma((nr // 2,)), dma((nr // 2,)),
             dma((nc,)), dma((nc,)), dma((nr * nc,)), dma((nr * nc,)),
         ],
-        compiler_params=pltpu.CompilerParams(collective_id=0, has_side_effects=True, vmem_limit_bytes=LIMIT),
+        compiler_params=pltpu.CompilerParams(collective_id=0, has_side_effects=True),
     )(vectors, tile_vals, flip(tile_rows), flip(tile_cols), tile_counts, flip(tile_diag)))
 
 
@@ -337,7 +336,7 @@
         in_specs=[pl.BlockSpec(memory_space=pltpu.VMEM)] * 2,
         out_specs=(pl.BlockSpec(memory_space=pltpu.MemorySpace.HBM),) * 2,
         scratch_shapes=[pltpu.SemaphoreType.DMA((2,))],
-        compiler_params=pltpu.CompilerParams(vmem_limit_bytes=LIMIT),
+        compiler_params=pltpu.CompilerParams(vmem_limit_bytes=2**20),
     )(applied, subspace)
 
 

time: 21.4 us -> 19 us (0.89)
  local copies, waits for them, and re-layouts: 2.37 us -> 0 us
    unnamed x12 -> x0, local copies, waits for them, and re-layouts: 2.37 us -> none
where the time goes in v5:
time: 19 us; the launch traced here: 18.9 us
  Pallas kernels  18.2 us (96%)
  between operations  0.64 us (3%)
    pallas_call x1, Pallas kernels, shards(): pl.pallas_call(functools.partial(kernel, nr, nc, scale), out_shape=(pltpu...  17.6 us
    pallas_call x1, Pallas kernels, finish(): pl.pallas_call(body, out_shape=(jax.ShapeDtypeStruct(applied.shape, appli...  0.62 us

profile of v5, /device:TPU:0, one launch (start us, length us, event | category | flops | bytes accessed | tf_op | source)
XLA Modules:
  0.0 18.9 jit_solution(11596502622972911025)
XLA Ops:
  0.6 17.6 %shard_map.77 = (f32[3,8,128]{2,1,0:T(8,128)S(1)}, f32[3,8,8]{2,1,0:T(8,128)S(1)}) custom-call(bf16[8,128]{1,0:T(8,128)(2,1)} %v_hbm.1, bf16[1,1,3,4,128,128]{5,4,3,2,1,0:T(8,128)(2,1)} %w_hbm.1, s32[1,3,1,4]{3,2,1,0:T(1,128)} %bitcast.3, s32[1,3,1,4]{3,2,1,0:T(1,128)} %bitcast.4, s32[1,1,3]{2,1,0:T(1,128)} %counts_hbm.1, s32[1,3,1,4]{3,2,1,0:T(1,128)} %bitcast.5), custom_call_target="tpu_custom_call" | custom-call | tf_op jit(solution)/shard_map/pallas_call | solution.py:287
  18.2 0.6 %shard_map.78 = (f32[3,8,128]{2,1,0:T(8,128)}, f32[3,8,8]{2,1,0:T(8,128)}) custom-call(f32[3,8,128]{2,1,0:T(8,128)S(1)} %get-tuple-element.4.a_ref, f32[3,8,8]{2,1,0:T(8,128)S(1)} %get-tuple-element.5.b_ref), custom_call_target="tpu_custom_call" | custom-call | tf_op jit(solution)/shard_map/pallas_call | solution.py:330

commit v6 on v5

--- a/solution.py
+++ b/solution.py
@@ -185,6 +185,20 @@
     each_device(lambda p: sp(p).start())
     srecv[me] = ssend[...]
 
+    def mp(j):
+        return remote(
+            msum.at[j], mrecv.at[q], m_send.at[j], m_recv.at[q], 2 * j + half, c
+        )
+
+    pp(0).wait_recv()
+    msum[0] = mpart[half, 0] + pair[0]
+
+    @pl.loop(1, q + 1)
+    def _(j):
+        pp(j).wait_recv()
+        msum[j] = mpart[half, j] + pair[j]
+        mp(j - 1).start()
+
     for t in range(terms):
         totals = [jnp.zeros((ev, width), jnp.float32) for _ in range(nc)]
         for k in range(slots):
@@ -201,20 +215,6 @@
 
     each_col(lambda p: fp(p).start())
     frecv[c] = fpart[c]
-
-    def mp(j):
-        return remote(
-            msum.at[j], mrecv.at[q], m_send.at[j], m_recv.at[q], 2 * j + half, c
-        )
-
-    pp(0).wait_recv()
-    msum[0] = mpart[half, 0] + pair[0]
-
-    @pl.loop(1, q + 1)
-    def _(j):
-        pp(j).wait_recv()
-        msum[j] = mpart[half, j] + pair[j]
-        mp(j - 1).start()
 
     each_col(
         lambda p: remote(fpart.at[p], frecv.at[p], f_send.at[p], f_recv.at[p], r, p).wait_recv()

time: 19 us -> 18.7 us (0.984)
  Pallas kernels: 18.2 us -> 17.9 us
    pallas_call x1, Pallas kernels: 17.6 us -> 17.3 us  [shards(): pl.pallas_call(functools.partial(kernel, nr, nc, scale), out_shape=(pltpu...]
where the time goes in v6:
time: 18.7 us; the launch traced here: 18.5 us
  Pallas kernels  17.9 us (96%)
  between operations  0.64 us (3%)
    pallas_call x1, Pallas kernels, shards(): pl.pallas_call(functools.partial(kernel, nr, nc, scale), out_shape=(pltpu...  17.3 us
    pallas_call x1, Pallas kernels, finish(): pl.pallas_call(body, out_shape=(jax.ShapeDtypeStruct(applied.shape, appli...  0.62 us

profile of v6, /device:TPU:0, one launch (start us, length us, event | category | flops | bytes accessed | tf_op | source)
XLA Modules:
  0.0 18.5 jit_solution(16718874537929871833)
XLA Ops:
  0.6 17.3 %shard_map.77 = (f32[3,8,128]{2,1,0:T(8,128)S(1)}, f32[3,8,8]{2,1,0:T(8,128)S(1)}) custom-call(bf16[8,128]{1,0:T(8,128)(2,1)} %v_hbm.1, bf16[1,1,3,4,128,128]{5,4,3,2,1,0:T(8,128)(2,1)} %w_hbm.1, s32[1,3,1,4]{3,2,1,0:T(1,128)} %bitcast.3, s32[1,3,1,4]{3,2,1,0:T(1,128)} %bitcast.4, s32[1,1,3]{2,1,0:T(1,128)} %counts_hbm.1, s32[1,3,1,4]{3,2,1,0:T(1,128)} %bitcast.5), custom_call_target="tpu_custom_call" | custom-call | tf_op jit(solution)/shard_map/pallas_call | solution.py:287
  17.9 0.6 %shard_map.78 = (f32[3,8,128]{2,1,0:T(8,128)}, f32[3,8,8]{2,1,0:T(8,128)}) custom-call(f32[3,8,128]{2,1,0:T(8,128)S(1)} %get-tuple-element.4.a_ref, f32[3,8,8]{2,1,0:T(8,128)S(1)} %get-tuple-element.5.b_ref), custom_call_target="tpu_custom_call" | custom-call | tf_op jit(solution)/shard_map/pallas_call | solution.py:330
